TPU v7x, 128 devices: a whole 4x4x4 slice. The times are simulated.
128 devices in a mesh: req: 16 (over x, z), mlp: 8 (over y, core).
Axes of the slice: x: 4, y: 4, z: 4, core: 2. Of those that a mesh axis runs over, the one named last changes fastest.
Arguments:
- patches: bfloat16 [15360, 4096], P('req'), may hold values from -6 to 6
- norm_gain: float32 [4096], replicated, may hold values from 0.25 to 1.75
- norm_bias: float32 [4096], replicated, may hold values from -3 to 3
- gate_weight: bfloat16 [4096, 8192], P(None, ('req', 'mlp')), may hold values from -0.09375 to 0.09375
- up_weight: bfloat16 [4096, 8192], P(None, ('req', 'mlp')), may hold values from -0.09375 to 0.09375
- down_weight: bfloat16 [4096, 8192], P(None, ('req', 'mlp')), may hold values from -0.0625 to 0.0625
- layer_scale: float32 [4096], replicated, may hold values from 0.25 to 2.5
- projection: bfloat16 [4, 4096, 4096], P(None, 'mlp', 'req'), may hold values from -0.046875 to 0.046875
- text_rows: bfloat16 [65536, 4096], P(('req', 'mlp')), may hold values from -6 to 6
- destination: int32 [3840], replicated, may hold values from -1 to 65535, as said below
Outputs:
- patch_out: bfloat16 [15360, 4096], P('req', 'mlp')
- streams: bfloat16 [65536, 4096], P(('req', 'mlp'))
Inputs may be any that keep to these rules, and one draw needn't show every extreme that they name: `destination`: values other than -1 are distinct positions; the positions landing in one piece of 512 consecutive positions (a stream holds 8 pieces) form one run of consecutive positions, at least one and at most 30 of them, and some piece receives exactly 30.
All inputs are finite; a program needn't handle non-finite values.
Results may differ from a plain program's by a relative error of at most 0.015.
Values may be sent and summed in bfloat16 or wider, within the bound.
No kernel may reach another device: no remote copies, remote signals or barrier semaphores. Data moves between devices by JAX's collectives and lax.ppermute only.
A program may use at most 128 MiB of HBM per device.

v0:
```python
import jax
import jax.numpy as jnp
from jax import lax
from jax.sharding import PartitionSpec as P


def layer_norm(values, norm_gain, norm_bias):
    row_mean = jnp.mean(values, axis=-1, keepdims=True)
    centred = values - row_mean
    variance = jnp.mean(centred * centred, axis=-1, keepdims=True)
    return centred * lax.rsqrt(variance + 1e-06) * norm_gain + norm_bias


def shards(
    patches,
    norm_gain,
    norm_bias,
    gate_weight,
    up_weight,
    down_weight,
    layer_scale,
    projection,
    text_rows,
    destination,
):
    req_count = lax.axis_size("req")
    mlp_count = lax.axis_size("mlp")
    req_index = lax.axis_index("req")
    mlp_index = lax.axis_index("mlp")
    rows_here, model_width = patches.shape
    feat_width = model_width // mlp_count
    inputs = patches.astype(jnp.float32)
    normed = layer_norm(inputs, norm_gain, norm_bias).astype(jnp.bfloat16)
    gate_act = jnp.dot(
        normed,
        lax.all_gather(gate_weight, "req", axis=1, tiled=True),
        preferred_element_type=jnp.float32,
    )
    up_act = jnp.dot(
        normed,
        lax.all_gather(up_weight, "req", axis=1, tiled=True),
        preferred_element_type=jnp.float32,
    )
    hidden = (jax.nn.silu(gate_act) * up_act).astype(jnp.bfloat16)
    ffn_local = lax.dot_general(
        hidden,
        lax.all_gather(down_weight, "req", axis=1, tiled=True),
        (((1,), (1,)), ((), ())),
        preferred_element_type=jnp.float32,
    )
    partial_value = lax.optimization_barrier(ffn_local.astype(jnp.bfloat16)).astype(jnp.float32)
    ffn_feats = lax.psum_scatter(
        partial_value.astype(jnp.bfloat16), "mlp", scatter_dimension=1, tiled=True
    ).astype(jnp.float32)
    scale_here = lax.dynamic_slice_in_dim(layer_scale, mlp_index * feat_width, feat_width)
    own_inputs = lax.dynamic_slice_in_dim(inputs, mlp_index * feat_width, feat_width, axis=1)
    patch_out = (own_inputs + scale_here * ffn_feats).astype(jnp.bfloat16)
    merged = patch_out.reshape(rows_here // 4, 4 * feat_width)
    weight_cols = projection.reshape(4 * feat_width, projection.shape[2])
    piece_rows = text_rows.shape[0]
    slot_count = destination.shape[0]
    bucket_count = req_count * mlp_count
    capacity = slot_count // bucket_count
    is_valid = destination >= 0
    piece_ids = jnp.where(is_valid, destination // piece_rows, -1)
    offsets = destination % piece_rows
    bucket_hit = piece_ids[:, None] == jnp.arange(bucket_count, dtype=jnp.int32)[None, :]
    first_off = jnp.min(jnp.where(bucket_hit, offsets[:, None], piece_rows), axis=0)
    counts = jnp.sum(bucket_hit.astype(jnp.int32), axis=0)
    slot_first = jnp.sum(jnp.where(bucket_hit, first_off[None, :], 0), axis=1)
    slot_rank = offsets - slot_first
    stream_ids = piece_ids // mlp_count
    piece_in = piece_ids % mlp_count
    rows_at = piece_in * (req_count * capacity) + stream_ids * capacity + slot_rank
    rows_at = jnp.where(is_valid, rows_at, bucket_count * capacity)
    sources = (
        jnp.full((bucket_count * capacity,), -1, jnp.int32)
        .at[rows_at]
        .set(jnp.arange(slot_count, dtype=jnp.int32), mode="drop")
    )
    every_row = lax.all_gather(merged, "req", axis=0, tiled=True)
    picked_rows = jnp.take(every_row, jnp.maximum(sources, 0), axis=0)
    picked_rows = jnp.where(sources[:, None] >= 0, picked_rows, jnp.zeros_like(picked_rows))
    summed = lax.psum_scatter(
        jnp.dot(picked_rows, weight_cols, preferred_element_type=jnp.float32).astype(jnp.bfloat16),
        "mlp",
        scatter_dimension=0,
        tiled=True,
    )
    arrived = lax.all_to_all(summed, "req", split_axis=0, concat_axis=1, tiled=True)
    bucket_here = req_index * mlp_count + mlp_index
    start_here = first_off[bucket_here]
    count_here = counts[bucket_here]
    positions = jnp.arange(piece_rows, dtype=jnp.int32) - start_here
    inside = (positions >= 0) & (positions < count_here)
    image_rows = jnp.take(arrived, jnp.clip(positions, 0, capacity - 1), axis=0)
    streams = jnp.where(inside[:, None], image_rows, text_rows)
    return (patch_out, streams)


def solution(mesh):
    return jax.shard_map(
        shards,
        mesh=mesh,
        in_specs=(
            P("req", None),
            P(),
            P(),
            P(None, ("req", "mlp")),
            P(None, ("req", "mlp")),
            P(None, ("req", "mlp")),
            P(),
            P(None, "mlp", "req"),
            P(("req", "mlp"), None),
            P(),
        ),
        out_specs=(P("req", "mlp"), P(("req", "mlp"), None)),
        check_vma=False,
    )
```

profile of v0, /device:TPU:0, one launch (start us, length us, event | category | flops | bytes accessed | tf_op | source)
XLA Modules:
  0.0 527.9 jit_solution(9855831558795438825)
XLA Ops:
  9.5 4.5 convert_reduce_fusion
  14.9 2.2 multiply_reduce_fusion
  17.1 66.4 %all-gather.5.cloned.1.call-done = bf16[4096,1024]{0,1:T(8,128)(2,1)} async-done(((bf16[4096,64]{0,1:T(8,128)(2,1)}), bf16[4096,1024]{0,1:T(8,128)(2,1)}) %all-gather.5.cloned.1.call-update) | async-done | bytes 8388624 | tf_op jit(solution)/shard_map/all_gather | solution.py:36
  83.5 14.4 %fusion.31 = f32[960,1024]{1,0:T(8,128)} fusion(bf16[4096,1024]{0,1:T(8,128)(2,1)} %all-gather.5.cloned.1.call-done, bf16[960,4096]{1,0:T(8,128)(2,1)} %param.10, f32[4096]{0:T(1024)S(1)} %copy-done.4, f32[4096]{0:T(1024)S(1)} %copy-done.5, f32[960]{0:T(1024)S(1)} %add_rsqrt_fusion, f32[960]{0:T(1024)S(1)} %broadcast_multiply_fusion), kind=kOutput, calls=%fused_computation.68 | convolution fusion | flops 8076656640 | bytes 20225536 | tf_op jit(solution)/shard_map/dot_general | solution.py:34
  97.9 58.2 %all-gather.7.cloned.1.call-done = bf16[4096,1024]{0,1:T(8,128)(2,1)} async-done(((bf16[4096,64]{0,1:T(8,128)(2,1)}), bf16[4096,1024]{0,1:T(8,128)(2,1)}) %all-gather.7.cloned.1.call-update) | async-done | bytes 8388624 | tf_op jit(solution)/shard_map/all_gather | solution.py:41
  156.1 72.6 %all-gather.9.cloned.1.call-done = bf16[4096,1024]{0,1:T(8,128)(2,1)} async-done(((bf16[4096,64]{0,1:T(8,128)(2,1)}), bf16[4096,1024]{0,1:T(8,128)(2,1)}) %all-gather.9.cloned.1.call-update) | async-done | bytes 8388624 | tf_op jit(solution)/shard_map/all_gather | solution.py:47
  228.7 25.9 %convolution_convert_fusion = bf16[960,4096]{1,0:T(8,128)(2,1)} fusion(bf16[4096,1024]{0,1:T(8,128)(2,1)} %all-gather.9.cloned.1.call-done, f32[960,1024]{1,0:T(8,128)} %fusion.31, bf16[4096,1024]{0,1:T(8,128)(2,1)} %all-gather.7.cloned.1.call-done, bf16[960,4096]{1,0:T(8,128)(2,1)} %param.10, f32[4096]{0:T(1024)S(1)} %copy-done.4, f32[4096]{0:T(1024)S(1)} %copy-done.5, ...), kind=kOutput, calls=%fused_computation.13 | convolution fusion | flops 16139550720 | bytes 36478464 | tf_op jit(solution)/shard_map/dot_general | solution.py:45
  254.7 11.3 %convert_element_type.26 = f32[960,4096]{1,0:T(8,128)} convert(bf16[960,4096]{1,0:T(8,128)(2,1)} %param.10) | non-fusion elementwise | flops 3932160 | bytes 23592960 | tf_op jit(solution)/shard_map/convert_element_type | solution.py:32
  266.7 37.6 %reduce-scatter.3.cloned.1.call-done = bf16[960,512]{1,0:T(8,128)(2,1)} async-done(((bf16[960,4096]{1,0:T(8,128)(2,1)}), bf16[960,512]{1,0:T(8,128)(2,1)}) %reduce-scatter.3.cloned.1.call-update) | async-done | bytes 983056 | tf_op jit(solution)/shard_map/reduce_scatter | solution.py:52
  304.3 2.2 add_convert_fusion.1
  306.5 1.5 reshape.67
  308.1 2.5 select_reduce_fusion.1
  310.6 2.4 convert_reduce_fusion.1
  313.1 14.6 %scatter_custom_fusion = s32[3840]{0:T(1024)S(1)} fusion(s32[3840]{0:T(1024)S(1)} %compare_select_fusion, s32[3840]{0:T(1024)S(1)} %iota.16, s32[]{:T(128)} %constant.104.clone.1), kind=kCustom, calls=%fused_computation.51 | custom fusion | bytes 15364 | tf_op jit(solution)/shard_map/scatter | solution.py:79
  327.7 86.2 %all-gather.11.cloned.1.call-done = bf16[3840,2048]{1,0:T(8,128)(2,1)} async-done(((bf16[240,2048]{1,0:T(8,128)(2,1)}), bf16[3840,2048]{1,0:T(8,128)(2,1)}) %all-gather.11.cloned.1.call-update) | async-done | bytes 15728656 | tf_op jit(solution)/shard_map/all_gather | solution.py:81
  413.9 37.0 %gather_fusion = bf16[3840,2048]{1,0:T(8,128)(2,1)} fusion(bf16[3840,2048]{1,0:T(8,128)(2,1)} %all-gather.11.cloned.1.call-done, s32[4096]{0:T(1024)S(1)} %pad_clamp_fusion), kind=kCustom, calls=%fused_computation | custom fusion | bytes 31472640 | tf_op jit(solution)/shard_map/jit(_take)/gather | solution.py:82
  450.9 9.9 %fusion.7 = bf16[3840,256]{1,0:T(8,128)(2,1)} fusion(bf16[2048,256]{1,0:T(8,128)(2,1)S(1)} %bitcast.13, bf16[3840,2048]{1,0:T(8,128)(2,1)} %gather_fusion, pred[3840]{0:T(1024)(128)(4,1)S(1)} %get-tuple-element.5, pred[3840]{0:T(1024)(128)(4,1)S(1)} %get-tuple-element.4), kind=kOutput, calls=%fused_computation.14 | convolution fusion | flops 4043243520 | bytes 18750976 | tf_op jit(solution)/shard_map/dot_general | solution.py:85
  462.1 31.9 %reduce-scatter.5.cloned.1.call-done = bf16[480,256]{1,0:T(8,128)(2,1)} async-done(((bf16[3840,256]{1,0:T(8,128)(2,1)}), bf16[480,256]{1,0:T(8,128)(2,1)}) %reduce-scatter.5.cloned.1.call-update) | async-done | bytes 245776 | tf_op jit(solution)/shard_map/reduce_scatter | solution.py:84
  494.0 1.7 all_to_all.14
  495.7 6.9 %all-to-all-start = ((bf16[16,30,256]{2,1,0:T(8,128)(2,1)}), bf16[16,30,256]{2,1,0:T(8,128)(2,1)S(1)}, u32[]{:S(2)}, u32[]{:S(2)}) async-start(bf16[16,30,256]{2,1,0:T(8,128)(2,1)} %all_to_all.14), calls=%async_computation.2 | async-start | bytes 524288 | tf_op jit(solution)/shard_map/all_to_all | solution.py:90
  502.6 1.3 fusion.27
  504.6 6.5 %all-to-all-done = bf16[16,30,256]{2,1,0:T(8,128)(2,1)S(1)} async-done(((bf16[16,30,256]{2,1,0:T(8,128)(2,1)}), bf16[16,30,256]{2,1,0:T(8,128)(2,1)S(1)}, u32[]{:S(2)}, u32[]{:S(2)}) %all-to-all-start) | async-done | bytes 245792 | tf_op jit(solution)/shard_map/all_to_all | solution.py:90
  511.4 4.4 gather_fusion.1
  515.7 5.3 select_select_fusion
  (40 shorter events, 6.4 us)
Async XLA Ops:
  7.2 443.7 %copy-start = (bf16[4,512,256]{2,1,0:T(8,128)(2,1)S(1)}, bf16[4,512,256]{2,1,0:T(8,128)(2,1)}, u32[]{:S(2)}) copy-start(bf16[4,512,256]{2,1,0:T(8,128)(2,1)} %param.17) | copy-start | bytes 3145732
  7.2 76.3 %all-gather.5.cloned.1.call-start = ((), (), s32[]{:S(2)}) async-start(), calls=%async_computation.3 | async-start | bytes 8912896 | tf_op jit(solution)/shard_map/all_gather | solution.py:36
  7.9 148.2 %all-gather.7.cloned.1.call-start = ((), (), s32[]{:S(2)}) async-start(), calls=%async_computation.4 | async-start | bytes 8912896 | tf_op jit(solution)/shard_map/all_gather | solution.py:41
  8.7 220.1 %all-gather.9.cloned.1.call-start = ((), (), s32[]{:S(2)}) async-start(), calls=%async_computation.5 | async-start | bytes 8912896 | tf_op jit(solution)/shard_map/all_gather | solution.py:47
  9.4 294.9 %reduce-scatter.3.cloned.1.call-start = ((), (), s32[]{:S(2)}) async-start(), calls=%async_computation.6 | async-start | bytes 8847360 | tf_op jit(solution)/shard_map/reduce_scatter | solution.py:52
  9.4 5.5 %copy-start.1 = (bf16[960,4096]{1,0:T(8,128)(2,1)S(1)}, bf16[960,4096]{1,0:T(8,128)(2,1)}, u32[]{:S(2)}) copy-start(bf16[960,4096]{1,0:T(8,128)(2,1)} %param.10) | copy-start | bytes 23592964
  9.5 74.1 %copy-start.4 = (f32[4096]{0:T(1024)S(1)}, f32[4096]{0:T(1024)}, u32[]{:S(2)}) copy-start(f32[4096]{0:T(1024)} %param.12) | copy-start | bytes 49156
  9.5 74.1 %copy-start.5 = (f32[4096]{0:T(1024)S(1)}, f32[4096]{0:T(1024)}, u32[]{:S(2)}) copy-start(f32[4096]{0:T(1024)} %param.11) | copy-start | bytes 49156
  254.6 159.3 %all-gather.11.cloned.1.call-start = ((), (), s32[]{:S(2)}) async-start(), calls=%async_computation.7 | async-start | bytes 16711680 | tf_op jit(solution)/shard_map/all_gather | solution.py:81
  254.7 53.4 %copy-start.3 = (s32[3840]{0:T(1024)S(1)}, s32[3840]{0:T(1024)}, u32[]{:S(2)}) copy-start(s32[3840]{0:T(1024)} %param.19) | copy-start | bytes 46084
  306.5 144.4 %copy-start.2 = (bf16[960,512]{1,0:T(8,128)(2,1)}, bf16[960,512]{1,0:T(8,128)(2,1)S(1)}, u32[]{:S(2)}) copy-start(bf16[960,512]{1,0:T(8,128)(2,1)S(1)} %add_convert_fusion.1) | copy-start | bytes 2949124
  308.0 186.0 %reduce-scatter.5.cloned.1.call-start = ((), (), s32[]{:S(2)}) async-start(), calls=%async_computation.8 | async-start | bytes 2211840 | tf_op jit(solution)/shard_map/reduce_scatter | solution.py:84
  495.7 15.4 %all-to-all-start = ((bf16[16,30,256]{2,1,0:T(8,128)(2,1)}), bf16[16,30,256]{2,1,0:T(8,128)(2,1)S(1)}, u32[]{:S(2)}, u32[]{:S(2)}) async-start(bf16[16,30,256]{2,1,0:T(8,128)(2,1)} %all_to_all.14), calls=%async_computation.2 | async-start | bytes 524288 | tf_op jit(solution)/shard_map/all_to_all | solution.py:90
Sparse Core Ops, SparseCore 0:
  10.2 73.3 all-gather.4
  85.7 70.4 all-gather.6
  158.3 70.4 all-gather.8
  254.7 49.5 reduce-scatter.2
  308.2 105.6 all-gather.10
  460.9 33.0 reduce-scatter.4
where the time goes:
time: 528 us
  waiting for transfers between devices  362 us (69%)
  local copies, waits for them, and re-layouts  62.5 us (12%)
  matrix products  50.1 us (9%)
  other arithmetic  32.3 us (6%)
  between operations  14.3 us (3%)
  starting transfers between devices  7.14 us (1%)
    all_gather x1, waiting for transfers between devices, shards(): every_row = lax.all_gather(merged, 'req', axis=0, tiled=True)  86.2 us
    all_gather x1, waiting for transfers between devices, shards(): lax.all_gather(down_weight, 'req', axis=1, tiled=True)  72.6 us
    all_gather x1, waiting for transfers between devices, shards(): lax.all_gather(gate_weight, 'req', axis=1, tiled=True)  66.4 us
    all_gather x1, waiting for transfers between devices, shards(): lax.all_gather(up_weight, 'req', axis=1, tiled=True)  58.2 us
    reduce_scatter x1, waiting for transfers between devices, shards(): lax.psum_scatter(partial_value.astype(jnp.bfloat16), 'mlp', scatter_dimen...  37.6 us
    gather x1, local copies, waits for them, and re-layouts, shards(): picked_rows = jnp.take(every_row, jnp.maximum(sources, 0), axis=0)  37 us
    reduce_scatter x1, waiting for transfers between devices, shards(): lax.psum_scatter(jnp.dot(picked_rows, weight_cols, preferred_element_type...  31.9 us
    dot_general x1, matrix products, shards(): lax.dot_general(hidden, lax.all_gather(down_weight, 'req', axis=1, tiled=...  25.9 us
  transfers between devices with their start and end apart: 7, of which 7 were waited for; matrix products, arithmetic and copies ran while one was open for 11% of the time, Pallas kernels for 0%

commit v1 on v0

--- a/solution.py
+++ b/solution.py
@@ -33,7 +33,9 @@
     normed = layer_norm(inputs, norm_gain, norm_bias).astype(jnp.bfloat16)
     gate_act = jnp.dot(
         normed,
-        lax.all_gather(gate_weight, "req", axis=1, tiled=True),
+        jnp.concatenate(
+            lax.all_to_all(jnp.stack([gate_weight] * lax.axis_size("req")), "req", 0, 0), axis=1
+        ),
         preferred_element_type=jnp.float32,
     )
     up_act = jnp.dot(

time: 528 us -> 570 us (1.080)
  waiting for transfers between devices: 362 us -> 387 us
  starting transfers between devices: 7.14 us -> 15.2 us
    all_to_all x0 -> x1, waiting for transfers between devices: none -> 143 us  [shards(): lax.all_to_all(jnp.stack([gate_weight] * lax.axis_size('req')), 'req', 0, 0)]
    all_gather x1 -> x0, waiting for transfers between devices: 66.4 us -> none  [shards(): lax.all_gather(gate_weight, 'req', axis=1, tiled=True)]
    all_gather x1, waiting for transfers between devices: 58.2 us -> 5.99 us  [shards(): lax.all_gather(up_weight, 'req', axis=1, tiled=True)]
    all_to_all x0 -> x1, starting transfers between devices: none -> 8.01 us  [shards(): lax.all_to_all(jnp.stack([gate_weight] * lax.axis_size('req')), 'req', 0, 0)]
where the time goes in v1:
time: 570 us; the launch traced here: 569 us
  waiting for transfers between devices  387 us (68%)
  local copies, waits for them, and re-layouts  66.7 us (12%)
  matrix products  50.4 us (9%)
  other arithmetic  35.6 us (6%)
  starting transfers between devices  15.2 us (3%)
  between operations  14 us (2%)
    all_to_all x1, waiting for transfers between devices, shards(): lax.all_to_all(jnp.stack([gate_weight] * lax.axis_size('req')), 'req', 0, 0)  143 us
    all_gather x1, waiting for transfers between devices, shards(): every_row = lax.all_gather(merged, 'req', axis=0, tiled=True)  86.2 us
    all_gather x1, waiting for transfers between devices, shards(): lax.all_gather(down_weight, 'req', axis=1, tiled=True)  74.8 us
    reduce_scatter x1, waiting for transfers between devices, shards(): lax.psum_scatter(partial_value.astype(jnp.bfloat16), 'mlp', scatter_dimen...  37.6 us
    gather x1, local copies, waits for them, and re-layouts, shards(): picked_rows = jnp.take(every_row, jnp.maximum(sources, 0), axis=0)  37 us
    reduce_scatter x1, waiting for transfers between devices, shards(): lax.psum_scatter(jnp.dot(picked_rows, weight_cols, preferred_element_type...  31.9 us
    dot_general x1, matrix products, shards(): lax.dot_general(hidden, lax.all_gather(down_weight, 'req', axis=1, tiled=...  25.9 us
    scatter x1, local copies, waits for them, and re-layouts, shards(): sources = jnp.full((bucket_count * capacity,), -1, jnp.int32).at[rows_at]...  14.6 us
  transfers between devices with their start and end apart: 7, of which 7 were waited for; matrix products, arithmetic and copies ran while one was open for 11% of the time, Pallas kernels for 0%

profile of v1, /device:TPU:0, one launch (start us, length us, event | category | flops | bytes accessed | tf_op | source)
XLA Modules:
  0.0 568.9 jit_solution(251003677645856364)
XLA Ops:
  8.7 5.3 stack.2
  14.0 8.0 %all-to-all-start = ((bf16[16,4096,64]{1,2,0:T(8,128)(2,1)}), bf16[16,4096,64]{1,2,0:T(8,128)(2,1)}, u32[]{:S(2)}, u32[]{:S(2)}) async-start(bf16[16,4096,64]{1,2,0:T(8,128)(2,1)} %stack.2), calls=%async_computation | async-start | bytes 16777216 | tf_op jit(solution)/shard_map/all_to_all | solution.py:37
  22.1 4.6 convert_reduce_fusion
  26.7 5.4 multiply_reduce_fusion
  32.2 142.6 %all-to-all-done = bf16[16,4096,64]{1,2,0:T(8,128)(2,1)} async-done(((bf16[16,4096,64]{1,2,0:T(8,128)(2,1)}), bf16[16,4096,64]{1,2,0:T(8,128)(2,1)}, u32[]{:S(2)}, u32[]{:S(2)}) %all-to-all-start) | async-done | bytes 8388640 | tf_op jit(solution)/shard_map/all_to_all | solution.py:37
  174.7 14.6 %fusion.31 = f32[960,1024]{1,0:T(8,128)} fusion(bf16[4096,1024]{0,1:T(8,128)(2,1)} %bitcast.1, bf16[960,4096]{1,0:T(8,128)(2,1)} %param.10, f32[4096]{0:T(1024)S(1)} %copy-done.3, f32[4096]{0:T(1024)S(1)} %copy-done.4, f32[960]{0:T(1024)S(1)} %add_rsqrt_fusion, f32[960]{0:T(1024)S(1)} %broadcast_multiply_fusion), kind=kOutput, calls=%fused_computation.68 | convolution fusion | flops 8076656640 | bytes 20225536 | tf_op jit(solution)/shard_map/dot_general | solution.py:34
  189.3 6.0 %all-gather.4.cloned.1.call-done = bf16[4096,1024]{0,1:T(8,128)(2,1)} async-done(((bf16[4096,64]{0,1:T(8,128)(2,1)}), bf16[4096,1024]{0,1:T(8,128)(2,1)}) %all-gather.4.cloned.1.call-update) | async-done | bytes 8388624 | tf_op jit(solution)/shard_map/all_gather | solution.py:43
  195.3 74.8 %all-gather.6.cloned.1.call-done = bf16[4096,1024]{0,1:T(8,128)(2,1)} async-done(((bf16[4096,64]{0,1:T(8,128)(2,1)}), bf16[4096,1024]{0,1:T(8,128)(2,1)}) %all-gather.6.cloned.1.call-update) | async-done | bytes 8388624 | tf_op jit(solution)/shard_map/all_gather | solution.py:49
  270.1 25.9 %convolution_convert_fusion = bf16[960,4096]{1,0:T(8,128)(2,1)} fusion(bf16[4096,1024]{0,1:T(8,128)(2,1)} %all-gather.6.cloned.1.call-done, f32[960,1024]{1,0:T(8,128)} %fusion.31, bf16[4096,1024]{0,1:T(8,128)(2,1)} %all-gather.4.cloned.1.call-done, bf16[960,4096]{1,0:T(8,128)(2,1)} %param.10, f32[4096]{0:T(1024)S(1)} %copy-done.3, f32[4096]{0:T(1024)S(1)} %copy-done.4, ...), kind=kOutput, calls=%fused_computation.13 | convolution fusion | flops 16139550720 | bytes 36478464 | tf_op jit(solution)/shard_map/dot_general | solution.py:47
  296.0 11.3 %convert_element_type.26 = f32[960,4096]{1,0:T(8,128)} convert(bf16[960,4096]{1,0:T(8,128)(2,1)} %param.10) | non-fusion elementwise | flops 3932160 | bytes 23592960 | tf_op jit(solution)/shard_map/convert_element_type | solution.py:32
  308.1 37.6 %reduce-scatter.3.cloned.1.call-done = bf16[960,512]{1,0:T(8,128)(2,1)} async-done(((bf16[960,4096]{1,0:T(8,128)(2,1)}), bf16[960,512]{1,0:T(8,128)(2,1)}) %reduce-scatter.3.cloned.1.call-update) | async-done | bytes 983056 | tf_op jit(solution)/shard_map/reduce_scatter | solution.py:54
  345.7 2.2 add_convert_fusion.1
  349.5 2.5 select_reduce_fusion.1
  352.0 2.4 convert_reduce_fusion.1
  354.4 14.6 %scatter_custom_fusion = s32[3840]{0:T(1024)S(1)} fusion(s32[3840]{0:T(1024)S(1)} %compare_select_fusion, s32[3840]{0:T(1024)S(1)} %iota.16, s32[]{:T(128)} %constant.104.clone.1), kind=kCustom, calls=%fused_computation.51 | custom fusion | bytes 15364 | tf_op jit(solution)/shard_map/scatter | solution.py:81
  369.1 86.2 %all-gather.8.cloned.1.call-done = bf16[3840,2048]{1,0:T(8,128)(2,1)} async-done(((bf16[240,2048]{1,0:T(8,128)(2,1)}), bf16[3840,2048]{1,0:T(8,128)(2,1)}) %all-gather.8.cloned.1.call-update) | async-done | bytes 15728656 | tf_op jit(solution)/shard_map/all_gather | solution.py:83
  455.3 37.0 %gather_fusion = bf16[3840,2048]{1,0:T(8,128)(2,1)} fusion(bf16[3840,2048]{1,0:T(8,128)(2,1)} %all-gather.8.cloned.1.call-done, s32[4096]{0:T(1024)S(1)} %pad_clamp_fusion), kind=kCustom, calls=%fused_computation | custom fusion | bytes 31472640 | tf_op jit(solution)/shard_map/jit(_take)/gather | solution.py:84
  492.2 9.9 %fusion.7 = bf16[3840,256]{1,0:T(8,128)(2,1)} fusion(bf16[2048,256]{1,0:T(8,128)(2,1)S(1)} %bitcast.15, bf16[3840,2048]{1,0:T(8,128)(2,1)} %gather_fusion, pred[3840]{0:T(1024)(128)(4,1)S(1)} %get-tuple-element.5, pred[3840]{0:T(1024)(128)(4,1)S(1)} %get-tuple-element.4), kind=kOutput, calls=%fused_computation.14 | convolution fusion | flops 4043243520 | bytes 18750976 | tf_op jit(solution)/shard_map/dot_general | solution.py:87
  503.4 31.9 %reduce-scatter.5.cloned.1.call-done = bf16[480,256]{1,0:T(8,128)(2,1)} async-done(((bf16[3840,256]{1,0:T(8,128)(2,1)}), bf16[480,256]{1,0:T(8,128)(2,1)}) %reduce-scatter.5.cloned.1.call-update) | async-done | bytes 245776 | tf_op jit(solution)/shard_map/reduce_scatter | solution.py:86
  535.3 1.7 all_to_all.18
  537.0 7.0 %all-to-all-start.1 = ((bf16[16,30,256]{2,1,0:T(8,128)(2,1)}), bf16[16,30,256]{2,1,0:T(8,128)(2,1)S(1)}, u32[]{:S(2)}, u32[]{:S(2)}) async-start(bf16[16,30,256]{2,1,0:T(8,128)(2,1)} %all_to_all.18), calls=%async_computation.3 | async-start | bytes 524288 | tf_op jit(solution)/shard_map/all_to_all | solution.py:92
  545.8 6.7 %all-to-all-done.1 = bf16[16,30,256]{2,1,0:T(8,128)(2,1)S(1)} async-done(((bf16[16,30,256]{2,1,0:T(8,128)(2,1)}), bf16[16,30,256]{2,1,0:T(8,128)(2,1)S(1)}, u32[]{:S(2)}, u32[]{:S(2)}) %all-to-all-start.1) | async-done | bytes 245792 | tf_op jit(solution)/shard_map/all_to_all | solution.py:92
  552.7 4.4 gather_fusion.1
  557.1 5.3 select_select_fusion
  (38 shorter events, 7.2 us)
Async XLA Ops:
  7.2 485.1 %copy-start = (bf16[4,512,256]{2,1,0:T(8,128)(2,1)S(1)}, bf16[4,512,256]{2,1,0:T(8,128)(2,1)}, u32[]{:S(2)}) copy-start(bf16[4,512,256]{2,1,0:T(8,128)(2,1)} %param.17) | copy-start | bytes 3145732
  7.2 188.1 %all-gather.4.cloned.1.call-start = ((), (), s32[]{:S(2)}) async-start(), calls=%async_computation.4 | async-start | bytes 8912896 | tf_op jit(solution)/shard_map/all_gather | solution.py:43
  7.9 262.2 %all-gather.6.cloned.1.call-start = ((), (), s32[]{:S(2)}) async-start(), calls=%async_computation.5 | async-start | bytes 8912896 | tf_op jit(solution)/shard_map/all_gather | solution.py:49
  14.0 160.7 %all-to-all-start = ((bf16[16,4096,64]{1,2,0:T(8,128)(2,1)}), bf16[16,4096,64]{1,2,0:T(8,128)(2,1)}, u32[]{:S(2)}, u32[]{:S(2)}) async-start(bf16[16,4096,64]{1,2,0:T(8,128)(2,1)} %stack.2), calls=%async_computation | async-start | bytes 16777216 | tf_op jit(solution)/shard_map/all_to_all | solution.py:37
  22.0 152.7 %copy-start.3 = (f32[4096]{0:T(1024)S(1)}, f32[4096]{0:T(1024)}, u32[]{:S(2)}) copy-start(f32[4096]{0:T(1024)} %param.12) | copy-start | bytes 49156
  22.0 152.7 %copy-start.4 = (f32[4096]{0:T(1024)S(1)}, f32[4096]{0:T(1024)}, u32[]{:S(2)}) copy-start(f32[4096]{0:T(1024)} %param.11) | copy-start | bytes 49156
  22.0 323.6 %reduce-scatter.3.cloned.1.call-start = ((), (), s32[]{:S(2)}) async-start(), calls=%async_computation.6 | async-start | bytes 8847360 | tf_op jit(solution)/shard_map/reduce_scatter | solution.py:54
  296.0 159.3 %all-gather.8.cloned.1.call-start = ((), (), s32[]{:S(2)}) async-start(), calls=%async_computation.7 | async-start | bytes 16711680 | tf_op jit(solution)/shard_map/all_gather | solution.py:83
  296.0 53.4 %copy-start.2 = (s32[3840]{0:T(1024)S(1)}, s32[3840]{0:T(1024)}, u32[]{:S(2)}) copy-start(s32[3840]{0:T(1024)} %param.19) | copy-start | bytes 46084
  347.8 144.4 %copy-start.1 = (bf16[960,512]{1,0:T(8,128)(2,1)}, bf16[960,512]{1,0:T(8,128)(2,1)S(1)}, u32[]{:S(2)}) copy-start(bf16[960,512]{1,0:T(8,128)(2,1)S(1)} %add_convert_fusion.1) | copy-start | bytes 2949124
  349.4 185.9 %reduce-scatter.5.cloned.1.call-start = ((), (), s32[]{:S(2)}) async-start(), calls=%async_computation.8 | async-start | bytes 2211840 | tf_op jit(solution)/shard_map/reduce_scatter | solution.py:86
  537.0 15.5 %all-to-all-start.1 = ((bf16[16,30,256]{2,1,0:T(8,128)(2,1)}), bf16[16,30,256]{2,1,0:T(8,128)(2,1)S(1)}, u32[]{:S(2)}, u32[]{:S(2)}) async-start(bf16[16,30,256]{2,1,0:T(8,128)(2,1)} %all_to_all.18), calls=%async_computation.3 | async-start | bytes 524288 | tf_op jit(solution)/shard_map/all_to_all | solution.py:92
Sparse Core Ops, SparseCore 0:
  10.2 185.1 all-gather.3
  197.5 72.5 all-gather.5
  296.1 49.5 reduce-scatter.2
  349.5 105.6 all-gather.7
  502.3 32.9 reduce-scatter.4
